TPU v7x, 32 devices: a whole 2x2x4 slice. The times are simulated.
32 devices in a mesh: prow: 8 (over z, x), pcol: 4 (over y, core).
Axes of the slice: x: 2, y: 2, z: 4, core: 2. Of those that a mesh axis runs over, the one named last changes fastest.
Arguments:
- inverse_pool: float32 [1536, 1536], P('prow', 'pcol'), may hold values from -6 to 6
- panel_one: float32 [1536, 512], P(('prow', 'pcol')), may hold values from -0.1875 to 0.1875
- panel_two: float32 [1536, 512], P(('prow', 'pcol')), may hold values from -0.21875 to 0.21875
- upper_two: float32 [512, 512], replicated, may hold values from -0.25 to 0.25
- lower_one: float32 [512, 512], replicated, as said below
- lower_two: float32 [512, 512], replicated, as said below
- list_one: int32 [9], replicated, may hold values from 0 to 11, as said below
- list_two: int32 [6], replicated, may hold values from 0 to 11, as said below
Outputs:
- first_offdiag: float32 [1536, 512], P(('prow', 'pcol'))
- first_diag: float32 [512, 512], replicated
- second_offdiag: float32 [1536, 512], P(('prow', 'pcol'))
- second_coupling: float32 [512, 512], replicated
- second_diag: float32 [512, 512], replicated
Inputs may be any that keep to these rules, and one draw needn't show every extreme that they name: `list_one`: distinct block numbers, among them 0, 6 and 11. `list_two`: distinct block numbers, each of which is also in list_one, among them 0, 6 and 11. `lower_one`: lower triangular with a diagonal of 1 to 1.5. `lower_two`: lower triangular with a diagonal of 1 to 1.5.
All inputs are finite; a program needn't handle non-finite values.
Results may differ from a plain program's by a relative error of at most 0.000073.
Values sent between devices are 32-bit elements; how exact they have to be, the bound alone decides.
A program may use at most 64 MiB of HBM per device.

v0:
```python
import jax
import jax.numpy as jnp
from jax import lax
from jax.sharding import PartitionSpec as P

BLK = 128


def product(left, right):
    return jnp.dot(left, right, precision=lax.Precision.HIGHEST, preferred_element_type=jnp.float32)


def transposed_product(left, right):
    return lax.dot_general(
        left,
        right,
        (((0,), (0,)), ((), ())),
        precision=lax.Precision.HIGHEST,
        preferred_element_type=jnp.float32,
    )


def live_rows(listing, first_row, count):
    row_ids = first_row + lax.iota(jnp.int32, count)
    blocks = row_ids // BLK
    hits = jnp.any(blocks[:, None] == listing[None, :], axis=1)
    return jnp.where(hits, 1.0, 0.0).astype(jnp.float32)[:, None]


def multiply_ancestors(inverse_tile, masked_span):
    groups = lax.axis_size("prow") // lax.axis_size("pcol")
    columns = lax.axis_size("pcol")
    span_rows = masked_span.shape[0]
    stacked = lax.all_gather(masked_span, "prow", axis=0, tiled=True)
    grouped = stacked.reshape(columns, groups * span_rows, masked_span.shape[1])
    regrouped = lax.all_to_all(grouped, "pcol", split_axis=0, concat_axis=0, tiled=True)
    accumulated = jnp.einsum(
        "rjkm,kjmw->rw",
        inverse_tile.reshape(inverse_tile.shape[0], groups, columns, span_rows),
        regrouped.reshape(columns, groups, span_rows, masked_span.shape[1]),
        precision=lax.Precision.HIGHEST,
        preferred_element_type=jnp.float32,
    )
    return lax.psum_scatter(accumulated, "pcol", scatter_dimension=0, tiled=True)


def local(inverse_pool, panel_one, panel_two, upper_two, lower_one, lower_two, list_one, list_two):
    span_rows = panel_one.shape[0]
    span_index = lax.axis_index("prow") * lax.axis_size("pcol") + lax.axis_index("pcol")
    first_row = span_index * span_rows
    live_one = live_rows(list_one, first_row, span_rows)
    live_two = live_rows(list_two, first_row, span_rows)
    masked_one = live_one * panel_one
    masked_two = live_two * panel_two
    first_offdiag = -live_one * multiply_ancestors(inverse_pool, masked_one)
    first_terms, coupling_terms = lax.psum(
        (
            transposed_product(masked_one, first_offdiag),
            transposed_product(first_offdiag, masked_two),
        ),
        ("prow", "pcol"),
    )
    second_product = multiply_ancestors(inverse_pool, masked_two)
    second_offdiag = -live_two * (product(first_offdiag, upper_two) + second_product)
    last_terms = lax.psum(transposed_product(masked_two, second_offdiag), ("prow", "pcol"))
    first_diag = transposed_product(lower_one, lower_one) - first_terms
    second_coupling = -(product(first_diag, upper_two) + coupling_terms)
    second_diag = (
        transposed_product(lower_two, lower_two)
        - transposed_product(upper_two, second_coupling)
        - last_terms
    )
    return (first_offdiag, first_diag, second_offdiag, second_coupling, second_diag)


def solution(mesh):
    return jax.shard_map(
        local,
        mesh=mesh,
        in_specs=(
            P("prow", "pcol"),
            P(("prow", "pcol"), None),
            P(("prow", "pcol"), None),
            P(),
            P(),
            P(),
            P(),
            P(),
        ),
        out_specs=(P(("prow", "pcol"), None), P(), P(("prow", "pcol"), None), P(), P()),
        check_vma=False,
    )
```

profile of v0, /device:TPU:0, one launch (start us, length us, event | category | flops | bytes accessed | tf_op | source)
XLA Modules:
  0.0 291.4 jit_solution(14642631012527775425)
XLA Ops:
  7.2 0.0 copy-start
  7.2 0.0 copy-start.10
  7.2 0.7 copy-done.10
  7.9 0.1 compare_reduce_fusion
  8.0 1.0 broadcast_multiply_fusion.1
  9.0 35.9 %all_gather.6 = f32[384,512]{1,0:T(8,128)} all-gather(f32[48,512]{1,0:T(8,128)S(1)} %broadcast_multiply_fusion.1), channel_id=1, replica_groups=mesh['prow'=8,'pcol'=4] {'prow'}, dimensions={0}, use_global_device_ids=true | all-gather | bytes 884736 | tf_op jit(solution)/shard_map/all_gather | solution.py:34
  44.9 0.0 copy-start.8
  44.9 3.6 %all-to-all-start = ((f32[4,96,512]{2,1,0:T(8,128)}), f32[4,96,512]{2,1,0:T(8,128)S(1)}, u32[]{:S(2)}, u32[]{:S(2)}) async-start(f32[4,96,512]{2,1,0:T(8,128)} %bitcast), calls=%async_computation | async-start | bytes 1572864 | tf_op jit(solution)/shard_map/all_to_all | solution.py:36
  48.5 0.0 copy-start.11
  48.6 0.0 copy-start.9
  48.6 0.0 reduce-scatter.3.cloned.1.call-start
  48.6 0.0 copy-done.8
  48.6 0.2 copy.20
  48.8 0.4 copy-done.11
  49.2 0.1 compare_reduce_fusion.1
  49.3 0.2 copy-done.9
  49.5 0.1 broadcast_multiply_fusion
  49.5 10.6 %all-to-all-done = f32[4,96,512]{2,1,0:T(8,128)S(1)} async-done(((f32[4,96,512]{2,1,0:T(8,128)}), f32[4,96,512]{2,1,0:T(8,128)S(1)}, u32[]{:S(2)}, u32[]{:S(2)}) %all-to-all-start) | async-done | bytes 786464 | tf_op jit(solution)/shard_map/all_to_all | solution.py:36
  60.1 1.6 convolution_bitcast_fusion.2
  61.8 0.0 reduce-scatter.3.cloned.1.call-update
  61.8 0.0 reduce-scatter.5.cloned.1.call-start
  61.8 32.3 %all_gather.7 = f32[384,512]{1,0:T(8,128)S(1)} all-gather(f32[48,512]{1,0:T(8,128)S(1)} %broadcast_multiply_fusion), channel_id=1, replica_groups=mesh['prow'=8,'pcol'=4] {'prow'}, dimensions={0}, use_global_device_ids=true | all-gather | bytes 884736 | tf_op jit(solution)/shard_map/all_gather | solution.py:34
  94.1 14.0 %all_to_all.10 = f32[4,96,512]{2,1,0:T(8,128)S(1)} all-to-all(f32[4,96,512]{2,1,0:T(8,128)S(1)} %bitcast.45), channel_id=1, replica_groups=mesh['prow'=8,'pcol'=4] {'pcol'}, dimensions={0} | all-to-all | bytes 1572864 | tf_op jit(solution)/shard_map/all_to_all | solution.py:36
  108.2 1.6 convolution_bitcast_fusion.1
  109.8 0.0 reduce-scatter.5.cloned.1.call-update
  109.8 0.2 all-reduce.3.cloned.1.call-start
  110.0 0.0 reduce-scatter.3.cloned.1.call-done
  110.1 1.0 broadcast_multiply_fusion.2
  111.0 0.0 copy-start.4
  111.0 2.0 fusion.8
  113.0 2.0 fusion.9
  115.0 15.5 %reduce-scatter.5.cloned.1.call-done = f32[48,512]{1,0:T(8,128)} async-done(((f32[192,512]{1,0:T(8,128)}), f32[48,512]{1,0:T(8,128)}) %reduce-scatter.5.cloned.1.call-update) | async-done | bytes 98320 | tf_op jit(solution)/shard_map/reduce_scatter | solution.py:44
  130.6 0.0 copy-done.4
  130.6 0.0 copy-done
  130.6 1.6 fusion.3
  132.2 0.0 copy-start.7
  132.2 2.0 fusion.11
  134.2 0.0 copy-done.7
  134.2 0.0 copy-start.1
  134.2 0.0 all-reduce.3.cloned.1.call-update
  134.3 1.2 copy-done.1
  135.5 1.9 fusion.10
  137.3 138.8 %all-reduce.3.cloned.1.call-done = (f32[512,512]{1,0:T(8,128)}, f32[512,512]{1,0:T(8,128)}, f32[512,512]{1,0:T(8,128)}) async-done(((f32[512,512]{1,0:T(8,128)}, f32[512,512]{1,0:T(8,128)}, f32[512,512]{1,0:T(8,128)}), (f32[512,512]{1,0:T(8,128)}, f32[512,512]{1,0:T(8,128)}, f32[512,512]{1,0:T(8,128)})) %all-reduce.3.cloned.1.call-update) | async-done | bytes 3145744 | tf_op jit(solution)/shard_map/psum | solution.py:56
  276.2 0.0 copy-start.6
  276.2 3.8 %convolution_subtract_fusion = f32[512,512]{1,0:T(8,128)S(1)} fusion(f32[512,512]{1,0:T(8,128)} %get-tuple-element.5, f32[512,512]{1,0:T(8,128)} %param.12), kind=kOutput, calls=%fused_computation.5 | convolution fusion | flops 1610874880 | bytes 3145728 | tf_op jit(solution)/shard_map/dot_general | solution.py:14
  280.0 0.0 copy-start.3
  280.0 0.0 copy-done.6
  280.0 0.0 copy-start.5
  280.0 1.9 fusion.2
  282.0 0.0 copy-done.3
  282.0 0.0 copy-start.2
  282.0 0.0 copy-done.5
  282.0 2.9 fusion.1
  284.8 0.0 copy-done.2
  (3 shorter events, 0.0 us)
Async XLA Ops:
  7.2 123.4 %copy-start = (f32[512,512]{1,0:T(8,128)S(1)}, f32[512,512]{1,0:T(8,128)}, u32[]{:S(2)}) copy-start(f32[512,512]{1,0:T(8,128)} %param.11) | copy-start | bytes 3145732
  7.2 0.7 copy-start.10
  44.9 3.7 %copy-start.8 = (f32[192,384]{1,0:T(8,128)S(1)}, f32[192,384]{1,0:T(8,128)}, u32[]{:S(2)}) copy-start(f32[192,384]{1,0:T(8,128)} %param.8) | copy-start | bytes 884740
  44.9 15.2 %all-to-all-start = ((f32[4,96,512]{2,1,0:T(8,128)}), f32[4,96,512]{2,1,0:T(8,128)S(1)}, u32[]{:S(2)}, u32[]{:S(2)}) async-start(f32[4,96,512]{2,1,0:T(8,128)} %bitcast), calls=%async_computation | async-start | bytes 1572864 | tf_op jit(solution)/shard_map/all_to_all | solution.py:36
  48.5 0.7 copy-start.11
  48.6 0.9 copy-start.9
  48.6 61.5 %reduce-scatter.3.cloned.1.call-start = ((), (), s32[]{:S(2)}) async-start(), calls=%async_computation.4 | async-start | bytes 491520 | tf_op jit(solution)/shard_map/reduce_scatter | solution.py:44
  61.8 68.8 %reduce-scatter.5.cloned.1.call-start = ((), (), s32[]{:S(2)}) async-start(), calls=%async_computation.5 | async-start | bytes 491520 | tf_op jit(solution)/shard_map/reduce_scatter | solution.py:44
  109.8 166.4 %all-reduce.3.cloned.1.call-start = ((), (), s32[]{:S(2)}) async-start(), calls=%async_computation.6 | async-start | bytes 6291456 | tf_op jit(solution)/shard_map/psum | solution.py:56
  111.0 19.6 %copy-start.4 = (f32[48,512]{1,0:T(8,128)}, f32[48,512]{1,0:T(8,128)S(1)}, u32[]{:S(2)}) copy-start(f32[48,512]{1,0:T(8,128)S(1)} %broadcast_multiply_fusion.2) | copy-start | bytes 294916
  132.2 2.0 copy-start.7
  134.2 1.2 copy-start.1
  276.2 3.8 %copy-start.6 = (f32[512,512]{1,0:T(8,128)S(1)}, f32[512,512]{1,0:T(8,128)}, u32[]{:S(2)}) copy-start(f32[512,512]{1,0:T(8,128)} %get-tuple-element.6) | copy-start | bytes 3145732
  280.0 2.0 copy-start.3
  280.0 2.0 copy-start.5
  282.0 2.9 copy-start.2
Sparse Core Ops, SparseCore 0:
  61.9 20.7 reduce-scatter.2
  109.9 20.6 reduce-scatter.4
  137.0 139.1 all-reduce.2
where the time goes:
time: 292 us; the launch traced here: 291 us
  waiting for transfers between devices  165 us (57%)
  blocking collectives  82.2 us (28%)
  matrix products  21.3 us (7%)
  between operations  13.9 us (5%)
  starting transfers between devices  3.93 us (1%)
    psum x1, waiting for transfers between devices, local(): lax.psum((transposed_product(masked_one, first_offdiag), transposed_produ...  139 us
    all_gather x2, blocking collectives, multiply_ancestors(): stacked = lax.all_gather(masked_span, 'prow', axis=0, tiled=True)  68.2 us
    reduce_scatter x2, waiting for transfers between devices, multiply_ancestors(): lax.psum_scatter(accumulated, 'pcol', scatter_dimension=0, tiled=True)  15.6 us
    dot_general x6, matrix products, transposed_product(): lax.dot_general(left, right, (((0,), (0,)), ((), ())), precision=lax.Prec...  14.5 us
    all_to_all x1, blocking collectives, multiply_ancestors(): lax.all_to_all(grouped, 'pcol', split_axis=0, concat_axis=0, tiled=True)  14 us
    all_to_all x1, waiting for transfers between devices, multiply_ancestors(): lax.all_to_all(grouped, 'pcol', split_axis=0, concat_axis=0, tiled=True)  10.6 us
  transfers between devices with their start and end apart: 4, of which 3 were waited for; matrix products, arithmetic and copies ran while one was open for 3% of the time, Pallas kernels for 0%

commit v1 on v0

--- a/solution.py
+++ b/solution.py
@@ -2,6 +2,7 @@
 import jax.numpy as jnp
 from jax import lax
 from jax.sharding import PartitionSpec as P
+from jax.lax import psum
 
 BLK = 128
 
@@ -53,12 +54,15 @@
     masked_one = live_one * panel_one
     masked_two = live_two * panel_two
     first_offdiag = -live_one * multiply_ancestors(inverse_pool, masked_one)
-    first_terms, coupling_terms = lax.psum(
-        (
-            transposed_product(masked_one, first_offdiag),
-            transposed_product(first_offdiag, masked_two),
+    first_terms, coupling_terms = psum(
+        psum(
+            (
+                transposed_product(masked_one, first_offdiag),
+                transposed_product(first_offdiag, masked_two),
+            ),
+            "pcol",
         ),
-        ("prow", "pcol"),
+        "prow",
     )
     second_product = multiply_ancestors(inverse_pool, masked_two)
     second_offdiag = -live_two * (product(first_offdiag, upper_two) + second_product)

time: 292 us -> 424 us (1.45)
  waiting for transfers between devices: 165 us -> 287 us
  blocking collectives: 82.2 us -> 90.9 us
    psum x1 -> x3, waiting for transfers between devices: 139 us -> 235 us  [the longest x1 130 us: local(): lax.psum(transposed_product(masked_two, second_offdiag), ('prow', 'pcol'))]
    reduce_scatter x2, waiting for transfers between devices: 15.6 us -> 40.8 us  [multiply_ancestors(): lax.psum_scatter(accumulated, 'pcol', scatter_dimension=0, tiled=True)]
    all_to_all x1, blocking collectives: 14 us -> 22.9 us  [multiply_ancestors(): lax.all_to_all(grouped, 'pcol', split_axis=0, concat_axis=0, tiled=True)]
  transfers between devices with their start and end apart: 4 -> 6, of which waited for: 3 -> 6; matrix products, arithmetic and copies ran while one was open for 3% -> 3% of each run, Pallas kernels for 0% -> 0%
where the time goes in v1:
time: 424 us
  waiting for transfers between devices  287 us (68%)
  blocking collectives  90.9 us (21%)
  matrix products  21.8 us (5%)
  between operations  13.9 us (3%)
    psum x1, waiting for transfers between devices, local(): lax.psum(transposed_product(masked_two, second_offdiag), ('prow', 'pcol'))  130 us
    psum x1, waiting for transfers between devices, local(): psum(psum((transposed_product(masked_one, first_offdiag), transposed_prod...  102 us
    all_gather x2, blocking collectives, multiply_ancestors(): stacked = lax.all_gather(masked_span, 'prow', axis=0, tiled=True)  68.1 us
    reduce_scatter x2, waiting for transfers between devices, multiply_ancestors(): lax.psum_scatter(accumulated, 'pcol', scatter_dimension=0, tiled=True)  40.8 us
    all_to_all x1, blocking collectives, multiply_ancestors(): lax.all_to_all(grouped, 'pcol', split_axis=0, concat_axis=0, tiled=True)  22.9 us
    dot_general x6, matrix products, transposed_product(): lax.dot_general(left, right, (((0,), (0,)), ((), ())), precision=lax.Prec...  15.1 us
    all_to_all x1, waiting for transfers between devices, multiply_ancestors(): lax.all_to_all(grouped, 'pcol', split_axis=0, concat_axis=0, tiled=True)  11.4 us
  transfers between devices with their start and end apart: 6, of which 6 were waited for; matrix products, arithmetic and copies ran while one was open for 3% of the time, Pallas kernels for 0%

profile of v1, /device:TPU:0, one launch (start us, length us, event | category | flops | bytes accessed | tf_op | source)
XLA Modules:
  0.0 423.7 jit_solution(12090346021733940570)
XLA Ops:
  7.2 0.0 copy-start
  7.2 0.0 copy-start.10
  7.2 0.7 copy-done.10
  7.9 0.1 compare_reduce_fusion
  8.0 1.0 broadcast_multiply_fusion.1
  9.0 35.9 %all_gather.6 = f32[384,512]{1,0:T(8,128)} all-gather(f32[48,512]{1,0:T(8,128)S(1)} %broadcast_multiply_fusion.1), channel_id=1, replica_groups=mesh['prow'=8,'pcol'=4] {'prow'}, dimensions={0}, use_global_device_ids=true | all-gather | bytes 884736 | tf_op jit(solution)/shard_map/all_gather | solution.py:35
  44.9 0.0 copy-start.8
  44.9 3.6 all-to-all-start
  48.5 0.0 reduce-scatter.3.cloned.1.call-start
  48.6 0.0 copy-done.8
  48.6 0.2 copy.20
  48.8 11.4 %all-to-all-done = f32[4,96,512]{2,1,0:T(8,128)S(1)} async-done(((f32[4,96,512]{2,1,0:T(8,128)}), f32[4,96,512]{2,1,0:T(8,128)S(1)}, u32[]{:S(2)}, u32[]{:S(2)}) %all-to-all-start) | async-done | bytes 786464 | tf_op jit(solution)/shard_map/all_to_all | solution.py:37
  60.1 1.6 convolution_bitcast_fusion.2
  61.8 0.0 copy-start.11
  61.8 0.0 copy-start.9
  61.8 0.0 reduce-scatter.3.cloned.1.call-update
  61.8 0.0 all-reduce.10.cloned.1.call-start
  61.8 0.6 copy-done.11
  62.4 0.1 compare_reduce_fusion.1
  62.5 0.2 copy-done.9
  62.7 0.1 broadcast_multiply_fusion
  62.7 19.9 %reduce-scatter.3.cloned.1.call-done = f32[48,512]{1,0:T(8,128)} async-done(((f32[192,512]{1,0:T(8,128)}), f32[48,512]{1,0:T(8,128)}) %reduce-scatter.3.cloned.1.call-update) | async-done | bytes 98320 | tf_op jit(solution)/shard_map/reduce_scatter | solution.py:45
  82.7 1.0 broadcast_multiply_fusion.2
  83.6 0.0 copy-start.5
  83.6 2.0 fusion.8
  85.7 2.0 fusion.9
  87.7 0.0 all-reduce.10.cloned.1.call-update
  87.7 0.0 reduce-scatter.5.cloned.1.call-start
  87.7 32.2 %all_gather.7 = f32[384,512]{1,0:T(8,128)S(1)} all-gather(f32[48,512]{1,0:T(8,128)S(1)} %broadcast_multiply_fusion), channel_id=1, replica_groups=mesh['prow'=8,'pcol'=4] {'prow'}, dimensions={0}, use_global_device_ids=true | all-gather | bytes 884736 | tf_op jit(solution)/shard_map/all_gather | solution.py:35
  119.9 22.9 %all_to_all.10 = f32[4,96,512]{2,1,0:T(8,128)S(1)} all-to-all(f32[4,96,512]{2,1,0:T(8,128)S(1)} %bitcast.45), channel_id=1, replica_groups=mesh['prow'=8,'pcol'=4] {'pcol'}, dimensions={0} | all-to-all | bytes 1572864 | tf_op jit(solution)/shard_map/all_to_all | solution.py:37
  142.8 1.6 convolution_bitcast_fusion.1
  144.4 0.0 reduce-scatter.5.cloned.1.call-update
  144.4 0.0 all-reduce.8.cloned.1.call-start
  144.5 3.2 all-reduce.10.cloned.1.call-done
  147.6 0.0 copy-start.1
  147.6 0.0 all-reduce.8.cloned.1.call-update
  147.7 0.2 all-reduce.6.cloned.1.call-start
  147.9 1.0 copy-done.1
  148.9 1.9 fusion.10
  150.7 20.9 %reduce-scatter.5.cloned.1.call-done = f32[48,512]{1,0:T(8,128)} async-done(((f32[192,512]{1,0:T(8,128)}), f32[48,512]{1,0:T(8,128)}) %reduce-scatter.5.cloned.1.call-update) | async-done | bytes 98320 | tf_op jit(solution)/shard_map/reduce_scatter | solution.py:45
  171.6 0.0 copy-done.5
  171.6 0.0 copy-done
  171.6 1.6 fusion.3
  173.2 0.0 copy-start.7
  173.3 0.0 copy-start.2
  173.3 2.0 fusion.11
  175.3 0.0 copy-done.7
  175.3 0.0 all-reduce.6.cloned.1.call-update
  175.3 102.2 %all-reduce.8.cloned.1.call-done = (f32[512,512]{1,0:T(8,128)}, f32[512,512]{1,0:T(8,128)}) async-done(((f32[512,512]{1,0:T(8,128)}, f32[512,512]{1,0:T(8,128)}), (f32[512,512]{1,0:T(8,128)}, f32[512,512]{1,0:T(8,128)})) %all-reduce.8.cloned.1.call-update) | async-done | bytes 2097168 | tf_op jit(solution)/shard_map/psum | solution.py:57
  277.5 0.0 copy-done.2
  277.5 0.0 copy-start.6
  277.5 3.2 convolution_subtract_fusion
  280.6 0.0 copy-start.4
  280.7 1.0 copy-done.4
  281.6 0.0 copy-done.6
  281.6 1.8 fusion.2
  283.5 0.0 copy-start.3
  283.5 129.6 %all-reduce.6.cloned.1.call-done = f32[512,512]{1,0:T(8,128)} async-done(((f32[512,512]{1,0:T(8,128)}), f32[512,512]{1,0:T(8,128)}) %all-reduce.6.cloned.1.call-update) | async-done | bytes 1048592 | tf_op jit(solution)/shard_map/psum | solution.py:69
  413.1 4.1 fusion.1
  417.2 0.0 copy-done.3
  (3 shorter events, 0.0 us)
Async XLA Ops:
  7.2 164.5 %copy-start = (f32[512,512]{1,0:T(8,128)S(1)}, f32[512,512]{1,0:T(8,128)}, u32[]{:S(2)}) copy-start(f32[512,512]{1,0:T(8,128)} %param.11) | copy-start | bytes 3145732
  7.2 0.7 copy-start.10
  44.9 3.7 copy-start.8
  44.9 15.2 %all-to-all-start = ((f32[4,96,512]{2,1,0:T(8,128)}), f32[4,96,512]{2,1,0:T(8,128)S(1)}, u32[]{:S(2)}, u32[]{:S(2)}) async-start(f32[4,96,512]{2,1,0:T(8,128)} %bitcast), calls=%async_computation | async-start | bytes 1572864 | tf_op jit(solution)/shard_map/all_to_all | solution.py:37
  48.5 34.1 %reduce-scatter.3.cloned.1.call-start = ((), (), s32[]{:S(2)}) async-start(), calls=%async_computation.4 | async-start | bytes 491520 | tf_op jit(solution)/shard_map/reduce_scatter | solution.py:45
  61.8 0.7 copy-start.11
  61.8 0.9 copy-start.9
  61.8 85.8 %all-reduce.10.cloned.1.call-start = ((), (), s32[]{:S(2)}) async-start(), calls=%async_computation.8 | async-start | bytes 4194304 | tf_op jit(solution)/shard_map/psum | solution.py:58
  83.6 88.0 %copy-start.5 = (f32[48,512]{1,0:T(8,128)}, f32[48,512]{1,0:T(8,128)S(1)}, u32[]{:S(2)}) copy-start(f32[48,512]{1,0:T(8,128)S(1)} %broadcast_multiply_fusion.2) | copy-start | bytes 294916
  87.7 83.9 %reduce-scatter.5.cloned.1.call-start = ((), (), s32[]{:S(2)}) async-start(), calls=%async_computation.5 | async-start | bytes 491520 | tf_op jit(solution)/shard_map/reduce_scatter | solution.py:45
  144.4 133.0 %all-reduce.8.cloned.1.call-start = ((), (), s32[]{:S(2)}) async-start(), calls=%async_computation.7 | async-start | bytes 4194304 | tf_op jit(solution)/shard_map/psum | solution.py:57
  147.6 1.2 copy-start.1
  147.7 265.4 %all-reduce.6.cloned.1.call-start = ((), (), s32[]{:S(2)}) async-start(), calls=%async_computation.6 | async-start | bytes 2097152 | tf_op jit(solution)/shard_map/psum | solution.py:69
  173.2 2.0 copy-start.7
  173.3 104.2 %copy-start.2 = (f32[512,512]{1,0:T(8,128)S(1)}, f32[512,512]{1,0:T(8,128)}, u32[]{:S(2)}) copy-start(f32[512,512]{1,0:T(8,128)} %param.12) | copy-start | bytes 3145732
  277.5 4.2 copy-start.6
  280.6 1.0 copy-start.4
  283.5 133.7 %copy-start.3 = (f32[512,512]{1,0:T(8,128)}, f32[512,512]{1,0:T(8,128)S(1)}, u32[]{:S(2)}) copy-start(f32[512,512]{1,0:T(8,128)S(1)} %fusion.2) | copy-start | bytes 3145732
Sparse Core Ops, SparseCore 0:
  61.9 20.7 reduce-scatter.2
  87.8 59.7 all-reduce.9
  150.7 20.8 reduce-scatter.4
  175.1 102.2 all-reduce.7
  283.1 129.9 all-reduce.5
